TPU v7x, 32 devices: a whole 2x2x4 slice. The times are simulated.
32 devices in a mesh: row: 8 (over z, y), col: 4 (over x, core).
Axes of the slice: x: 2, y: 2, z: 4, core: 2. Of those that a mesh axis runs over, the one named last changes fastest.
Arguments:
- embeddings: bfloat16 [512, 1024], P(('row', 'col')), may hold values from -20 to 20
- group_ids: int32 [512], P(('row', 'col')), may hold values from 0 to 127, as said below
Outputs:
- loss: float32 [], replicated
- grad: bfloat16 [512, 1024], P(('row', 'col'))
Inputs may be any that keep to these rules, and one draw needn't show every extreme that they name: `group_ids`: every group id is held by exactly 4 rows, spread over the batch.
All inputs are finite; a program needn't handle non-finite values.
Results may differ from a plain program's by a relative error of at most 0.0045.
Values may be sent and summed in bfloat16 or wider, within the bound.
No kernel may reach another device: no remote copies, remote signals or barrier semaphores. Data moves between devices by JAX's collectives and lax.ppermute only.
A program may use at most 64 MiB of HBM per device.

v0:
```python
import jax
import jax.numpy as jnp
from jax import lax
from jax.sharding import PartitionSpec as P


def joined(part, axis, combine):
    gathered = jax.tree.map(lambda a: lax.all_gather(a, axis), part)

    def take(source):
        return jax.tree.map(lambda a: lax.dynamic_index_in_dim(a, source, 0, False), gathered)

    return lax.fori_loop(
        1, lax.axis_size(axis), lambda source, state: combine(state, take(source)), take(0)
    )


def combine_stats(first, second):
    peak = jnp.maximum(first[0], second[0])
    total = first[1] * jnp.exp(first[0] - peak) + second[1] * jnp.exp(second[0] - peak)
    return (peak, total, first[2] + second[2], first[3] + second[3])


def on_device(embeddings, group_ids):
    row_count = lax.axis_size("row")
    col_count = lax.axis_size("col")
    row_index = lax.axis_index("row")
    col_index = lax.axis_index("col")
    rows = embeddings.shape[0]
    width = embeddings.shape[1]
    scale = 1.0 / jnp.sqrt(jnp.float32(width))
    whole = rows * row_count * col_count
    queries, query_groups = (
        lax.all_gather(embeddings, "col", axis=0, tiled=True),
        lax.all_gather(group_ids, "col", axis=0, tiled=True),
    )
    keys, key_groups = (
        lax.all_gather(embeddings, "row", axis=0, tiled=True),
        lax.all_gather(group_ids, "row", axis=0, tiled=True),
    )
    query_len = rows * col_count
    key_len = rows * row_count
    query_pos = row_index * query_len + jnp.arange(query_len, dtype=jnp.int32)
    key_local = jnp.arange(key_len, dtype=jnp.int32)
    key_pos = (key_local // rows * col_count + col_index) * rows + key_local % rows
    scores = (
        lax.dot_general(queries, keys, (((1,), (1,)), ((), ())), preferred_element_type=jnp.float32)
        * scale
    )
    selfs = query_pos[:, None] == key_pos[None, :]
    positive = jnp.logical_and(query_groups[:, None] == key_groups[None, :], jnp.logical_not(selfs))
    masked = jnp.where(selfs, jnp.float32(-1e30), scores)
    peak = jnp.max(masked, axis=1)
    total = jnp.sum(jnp.exp(masked - peak[:, None]), axis=1)
    possum = jnp.sum(jnp.where(positive, scores, jnp.float32(0.0)), axis=1)
    count = jnp.sum(positive.astype(jnp.float32), axis=1)
    peak, total, possum, count = joined((peak, total, possum, count), "col", combine_stats)
    lse = peak + jnp.log(total)
    inverse = 1.0 / count
    row_loss = lse - possum * inverse
    own_start = col_index * rows
    own_loss = lax.dynamic_slice_in_dim(row_loss, own_start, rows, 0)
    loss = lax.psum(jnp.sum(own_loss), ("row", "col")) / whole
    weight = (
        jnp.exp(masked - lse[:, None]) - jnp.where(positive, inverse[:, None], jnp.float32(0.0))
    ) / whole
    weight = weight.astype(jnp.bfloat16)
    own_lse = lax.dynamic_slice_in_dim(lse, own_start, rows, 0)
    own_inverse = lax.dynamic_slice_in_dim(inverse, own_start, rows, 0)
    key_lse, key_inverse = (
        lax.all_gather(own_lse, "row", axis=0, tiled=True),
        lax.all_gather(own_inverse, "row", axis=0, tiled=True),
    )
    mirrored = (
        jnp.exp(masked - key_lse[None, :])
        - jnp.where(positive, key_inverse[None, :], jnp.float32(0.0))
    ) / whole
    mirrored = mirrored.astype(jnp.bfloat16)
    both_term = jnp.dot(weight, keys, preferred_element_type=jnp.float32) + jnp.dot(
        mirrored, keys, preferred_element_type=jnp.float32
    )
    grad = scale * lax.psum_scatter(both_term, "col", scatter_dimension=0, tiled=True)
    return (loss, grad.astype(jnp.bfloat16))


def solution(mesh):
    in_specs = (P(("row", "col"), None), P(("row", "col")))
    out_specs = (P(), P(("row", "col"), None))
    return jax.shard_map(
        on_device, mesh=mesh, in_specs=in_specs, out_specs=out_specs, check_vma=False
    )
```

profile of v0, /device:TPU:12, one launch (start us, length us, event | category | flops | bytes accessed | tf_op | source)
XLA Modules:
  0.0 142.9 jit_solution(13007018784665534406)
XLA Ops:
  7.2 0.0 reduce-scatter.2.cloned.1.call-start
  7.2 5.6 %all_gather.42 = bf16[64,1024]{1,0:T(8,128)(2,1)S(1)} all-gather(bf16[16,1024]{1,0:T(8,128)(2,1)} %param.4), channel_id=1, replica_groups=mesh['row'=8,'col'=4] {'col'}, dimensions={0}, use_global_device_ids=true | all-gather | bytes 163840 | tf_op jit(solution)/shard_map/all_gather | solution.py:34
  12.9 28.3 %all_gather.43 = bf16[128,1024]{1,0:T(8,128)(2,1)S(1)} all-gather(bf16[16,1024]{1,0:T(8,128)(2,1)S(1)} %copy-done), channel_id=1, replica_groups=mesh['row'=8,'col'=4] {'row'}, dimensions={0}, use_global_device_ids=true | all-gather | bytes 294912 | tf_op jit(solution)/shard_map/all_gather | solution.py:38
  41.1 0.6 copy-done.3
  41.8 0.7 dynamic-slice.3
  42.4 0.6 dynamic-slice
  45.0 0.6 copy-done.1
  45.7 0.2 dynamic-update-slice.2
  45.9 4.9 %all-reduce.2 = s32[64]{0:T(128)S(1)} all-reduce(s32[64]{0:T(128)S(1)} %dynamic-update-slice.2), channel_id=1, replica_groups=mesh['row'=8,'col'=4] {'col'}, use_global_device_ids=true, to_apply=%add.2 | all-reduce | flops 64 | bytes 512
  50.8 0.2 dynamic-update-slice.3
  51.0 11.3 %all-reduce.3 = s32[128]{0:T(128)S(1)} all-reduce(s32[128]{0:T(128)S(1)} %dynamic-update-slice.3), channel_id=1, replica_groups=mesh['row'=8,'col'=4] {'row'}, use_global_device_ids=true, to_apply=%add.3 | all-reduce | flops 128 | bytes 1024
  62.2 0.3 fusion.10
  62.5 0.2 dynamic-update-slice
  62.8 0.2 select_reduce_fusion
  63.0 0.2 dynamic-update-slice.5
  63.3 0.2 dynamic-update-slice.4
  63.5 0.2 dynamic-update-slice.1
  63.7 5.6 %all-reduce.9 = (f32[256]{0:T(256)S(1)}, f32[256]{0:T(256)S(1)}, f32[256]{0:T(256)S(1)}, f32[256]{0:T(256)S(1)}) all-reduce(f32[256]{0:T(256)S(1)} %dynamic-update-slice, f32[256]{0:T(256)S(1)} %dynamic-update-slice.1, f32[256]{0:T(256)S(1)} %dynamic-update-slice.4, f32[256]{0:T(256)S(1)} %dynamic-update-slice.5), channel_id=2, replica_groups=mesh['row'=8,'col'=4] {'col'}, use_global_device_ids=true, to_apply=%add | all-reduce | flops 1024 | bytes 8192
  69.3 0.1 reshape.42
  69.4 0.1 reshape.41
  69.5 0.1 reshape.40
  69.6 0.1 reshape.39
  69.6 0.2 while.21
  69.8 0.2 fusion.11
  70.1 0.2 dynamic-slice_dynamic-update-slice_fusion
  70.3 0.2 dynamic-slice_dynamic-update-slice_fusion.1
  70.4 17.1 %all-reduce.8 = (f32[128]{0:T(128)S(1)}, f32[128]{0:T(128)S(1)}) all-reduce(f32[128]{0:T(128)S(1)} %dynamic-slice_dynamic-update-slice_fusion, f32[128]{0:T(128)S(1)} %dynamic-slice_dynamic-update-slice_fusion.1), channel_id=1, replica_groups=mesh['row'=8,'col'=4] {'row'}, use_global_device_ids=true, to_apply=%add.7 | all-reduce | flops 256 | bytes 2048
  87.5 0.9 convolution_add_fusion
  88.5 0.7 dynamic-slice_reduce_fusion
  89.2 43.6 %psum.7 = f32[]{:T(128)} all-reduce(f32[]{:T(128)} %dynamic-slice_reduce_fusion), channel_id=1, replica_groups=mesh['row'=8,'col'=4] {'row','col'}, use_global_device_ids=true, to_apply=%region_7.8 | all-reduce | flops 1 | bytes 8 | tf_op jit(solution)/shard_map/psum | solution.py:63
  133.4 0.0 reduce-scatter.2.cloned.1.call-done
  133.5 1.5 %multiply_convert_fusion = bf16[16,1024]{1,0:T(8,128)(2,1)} fusion(f32[16,1024]{1,0:T(8,128)} %reduce-scatter.2.cloned.1.call-done), kind=kLoop, calls=%fused_computation.15 | loop fusion | flops 32768 | bytes 98304 | tf_op jit(solution)/shard_map/convert_element_type | solution.py:83
  (28 shorter events, 0.2 us)
Async XLA Ops:
  7.2 126.3 %reduce-scatter.2.cloned.1.call-start = ((), (), s32[]{:S(2)}) async-start(), calls=%async_computation.1 | async-start | bytes 327680 | tf_op jit(solution)/shard_map/reduce_scatter | solution.py:82
  7.2 5.6 %copy-start = (bf16[16,1024]{1,0:T(8,128)(2,1)S(1)}, bf16[16,1024]{1,0:T(8,128)(2,1)}, u32[]{:S(2)}) copy-start(bf16[16,1024]{1,0:T(8,128)(2,1)} %param.4) | copy-start | bytes 98308
  41.1 0.7 copy-start.3
  41.8 0.7 copy-start.2
  45.0 0.7 copy-start.1
Sparse Core Ops, SparseCore 0:
  88.6 20.8 reduce-scatter.1
where the time goes:
time: 143 us
  blocking collectives  116 us (81%)
  between operations  17.9 us (13%)
  local copies, waits for them, and re-layouts  4.48 us (3%)
  other arithmetic  2.51 us (2%)
  matrix products  1.48 us (1%)
    psum x1, blocking collectives, on_device(): loss = lax.psum(jnp.sum(own_loss), ('row', 'col')) / whole  43.6 us
    unnamed x4, blocking collectives  38.9 us
    all_gather x1, blocking collectives, on_device(): lax.all_gather(embeddings, 'row', axis=0, tiled=True)  28.3 us
    all_gather x1, blocking collectives, on_device(): lax.all_gather(embeddings, 'col', axis=0, tiled=True)  5.63 us
    unnamed x25, local copies, waits for them, and re-layouts  4.14 us
  transfers between devices with their start and end apart: 1, of which 0 were waited for; matrix products, arithmetic and copies ran while one was open for 0% of the time, Pallas kernels for 0%

commit v1 on v0

--- a/solution.py
+++ b/solution.py
@@ -35,7 +35,9 @@
         lax.all_gather(group_ids, "col", axis=0, tiled=True),
     )
     keys, key_groups = (
-        lax.all_gather(embeddings, "row", axis=0, tiled=True),
+        jnp.concatenate(
+            lax.all_to_all(jnp.stack([embeddings] * lax.axis_size("row")), "row", 0, 0), axis=0
+        ),
         lax.all_gather(group_ids, "row", axis=0, tiled=True),
     )
     query_len = rows * col_count

time: 143 us -> 120 us (0.84)
  blocking collectives: 116 us -> 86 us
  starting transfers between devices: 0.04 us -> 6.36 us
    all_gather x1 -> x0, blocking collectives: 28.3 us -> none  [on_device(): lax.all_gather(embeddings, 'row', axis=0, tiled=True)]
    all_to_all x0 -> x1, starting transfers between devices: none -> 6.35 us  [on_device(): lax.all_to_all(jnp.stack([embeddings] * lax.axis_size('row')), 'row', 0, 0)]
    another operation x0 -> x1, local copies, waits for them, and re-layouts: none -> 1.48 us  [on_device(): jnp.stack([embeddings] * lax.axis_size('row'))]
  transfers between devices with their start and end apart: 1 -> 2, of which waited for: 0 -> 0; matrix products, arithmetic and copies ran while one was open for 0% -> 2% of each run, Pallas kernels for 0% -> 0%
where the time goes in v1:
time: 120 us
  blocking collectives  86 us (72%)
  between operations  17.8 us (15%)
  starting transfers between devices  6.36 us (5%)
  local copies, waits for them, and re-layouts  5.32 us (4%)
  other arithmetic  2.51 us (2%)
  matrix products  1.48 us (1%)
    psum x1, blocking collectives, on_device(): loss = lax.psum(jnp.sum(own_loss), ('row', 'col')) / whole  43 us
    unnamed x4, blocking collectives  37.6 us
    all_to_all x1, starting transfers between devices, on_device(): lax.all_to_all(jnp.stack([embeddings] * lax.axis_size('row')), 'row', 0, 0)  6.35 us
    all_gather x1, blocking collectives, on_device(): lax.all_gather(embeddings, 'col', axis=0, tiled=True)  5.4 us
    unnamed x25, local copies, waits for them, and re-layouts  3.5 us
  transfers between devices with their start and end apart: 2, of which 0 were waited for; matrix products, arithmetic and copies ran while one was open for 2% of the time, Pallas kernels for 0%

profile of v1, /device:TPU:12, one launch (start us, length us, event | category | flops | bytes accessed | tf_op | source)
XLA Modules:
  0.0 119.6 jit_solution(8249292524868331445)
XLA Ops:
  7.2 1.5 %stack.2 = bf16[8,16,1024]{2,1,0:T(8,128)(2,1)} broadcast(bf16[16,1024]{1,0:T(8,128)(2,1)} %param.4), dimensions={1,2} | broadcast | bytes 294912 | tf_op jit(solution)/shard_map/stack | solution.py:39
  8.6 6.4 %all-to-all-start = ((bf16[8,16,1024]{2,1,0:T(8,128)(2,1)}), bf16[8,16,1024]{2,1,0:T(8,128)(2,1)S(1)}, u32[]{:S(2)}, u32[]{:S(2)}) async-start(bf16[8,16,1024]{2,1,0:T(8,128)(2,1)} %stack.2), calls=%async_computation | async-start | bytes 524288 | tf_op jit(solution)/shard_map/all_to_all | solution.py:39
  15.0 0.6 dynamic-slice.3
  15.7 0.6 dynamic-slice
  18.2 0.6 copy-done.1
  18.8 0.2 dynamic-update-slice.3
  19.0 0.2 dynamic-update-slice.2
  19.2 10.4 %all-reduce.3 = s32[128]{0:T(128)S(1)} all-reduce(s32[128]{0:T(128)S(1)} %dynamic-update-slice.3), channel_id=1, replica_groups=mesh['row'=8,'col'=4] {'row'}, use_global_device_ids=true, to_apply=%add.3 | all-reduce | flops 128 | bytes 1024
  29.6 4.9 %all-reduce.2 = s32[64]{0:T(128)S(1)} all-reduce(s32[64]{0:T(128)S(1)} %dynamic-update-slice.2), channel_id=1, replica_groups=mesh['row'=8,'col'=4] {'col'}, use_global_device_ids=true, to_apply=%add.2 | all-reduce | flops 64 | bytes 512
  34.5 5.4 %all_gather.39 = bf16[64,1024]{1,0:T(8,128)(2,1)S(1)} all-gather(bf16[16,1024]{1,0:T(8,128)(2,1)S(1)} %copy-done), channel_id=1, replica_groups=mesh['row'=8,'col'=4] {'col'}, dimensions={0}, use_global_device_ids=true | all-gather | bytes 163840 | tf_op jit(solution)/shard_map/all_gather | solution.py:34
  39.9 0.3 fusion.10
  40.2 0.2 dynamic-update-slice
  40.5 0.2 select_reduce_fusion
  40.7 0.2 dynamic-update-slice.5
  40.9 0.2 dynamic-update-slice.4
  41.2 0.2 dynamic-update-slice.1
  41.4 6.4 %all-reduce.9 = (f32[256]{0:T(256)S(1)}, f32[256]{0:T(256)S(1)}, f32[256]{0:T(256)S(1)}, f32[256]{0:T(256)S(1)}) all-reduce(f32[256]{0:T(256)S(1)} %dynamic-update-slice, f32[256]{0:T(256)S(1)} %dynamic-update-slice.1, f32[256]{0:T(256)S(1)} %dynamic-update-slice.4, f32[256]{0:T(256)S(1)} %dynamic-update-slice.5), channel_id=2, replica_groups=mesh['row'=8,'col'=4] {'col'}, use_global_device_ids=true, to_apply=%add | all-reduce | flops 1024 | bytes 8192
  47.8 0.1 reshape.45
  47.9 0.1 reshape.46
  48.0 0.1 reshape.47
  48.0 0.1 reshape.48
  48.1 0.2 while.21
  48.3 0.2 fusion.11
  48.6 0.2 dynamic-slice_dynamic-update-slice_fusion
  48.8 0.2 dynamic-slice_dynamic-update-slice_fusion.1
  48.9 15.9 %all-reduce.8 = (f32[128]{0:T(128)S(1)}, f32[128]{0:T(128)S(1)}) all-reduce(f32[128]{0:T(128)S(1)} %dynamic-slice_dynamic-update-slice_fusion, f32[128]{0:T(128)S(1)} %dynamic-slice_dynamic-update-slice_fusion.1), channel_id=1, replica_groups=mesh['row'=8,'col'=4] {'row'}, use_global_device_ids=true, to_apply=%add.7 | all-reduce | flops 256 | bytes 2048
  64.8 0.9 convolution_add_fusion
  65.7 0.0 reduce-scatter.2.cloned.1.call-update
  65.8 0.7 dynamic-slice_reduce_fusion
  66.4 43.0 %psum.7 = f32[]{:T(128)} all-reduce(f32[]{:T(128)} %dynamic-slice_reduce_fusion), channel_id=1, replica_groups=mesh['row'=8,'col'=4] {'row','col'}, use_global_device_ids=true, to_apply=%region_7.8 | all-reduce | flops 1 | bytes 8 | tf_op jit(solution)/shard_map/psum | solution.py:65
  110.1 0.0 reduce-scatter.2.cloned.1.call-done
  110.2 1.5 %multiply_convert_fusion = bf16[16,1024]{1,0:T(8,128)(2,1)} fusion(f32[16,1024]{1,0:T(8,128)} %reduce-scatter.2.cloned.1.call-done), kind=kLoop, calls=%fused_computation.15 | loop fusion | flops 32768 | bytes 98304 | tf_op jit(solution)/shard_map/convert_element_type | solution.py:85
  (30 shorter events, 0.2 us)
Async XLA Ops:
  8.6 6.4 %copy-start.3 = (u32[32]{0:T(128)S(1)}, u32[32]{0:T(128)}, u32[]{:S(2)}) copy-start(u32[32]{0:T(128)} %constant.134) | copy-start | bytes 388
  8.6 7.0 %copy-start.2 = (u32[32]{0:T(128)S(1)}, u32[32]{0:T(128)}, u32[]{:S(2)}) copy-start(u32[32]{0:T(128)} %constant.119) | copy-start | bytes 388
  8.6 31.3 %all-to-all-start = ((bf16[8,16,1024]{2,1,0:T(8,128)(2,1)}), bf16[8,16,1024]{2,1,0:T(8,128)(2,1)S(1)}, u32[]{:S(2)}, u32[]{:S(2)}) async-start(bf16[8,16,1024]{2,1,0:T(8,128)(2,1)} %stack.2), calls=%async_computation | async-start | bytes 524288 | tf_op jit(solution)/shard_map/all_to_all | solution.py:39
  15.0 19.5 %copy-start = (bf16[16,1024]{1,0:T(8,128)(2,1)S(1)}, bf16[16,1024]{1,0:T(8,128)(2,1)}, u32[]{:S(2)}) copy-start(bf16[16,1024]{1,0:T(8,128)(2,1)} %param.4) | copy-start | bytes 98308
  15.0 95.1 %reduce-scatter.2.cloned.1.call-start = ((), (), s32[]{:S(2)}) async-start(), calls=%async_computation.2 | async-start | bytes 327680 | tf_op jit(solution)/shard_map/reduce_scatter | solution.py:84
  18.2 0.7 copy-start.1
Sparse Core Ops, SparseCore 0:
  65.9 20.6 reduce-scatter.1
